TPU v7x, 32 devices: a whole 2x2x4 slice. The times are simulated.
32 devices in a mesh: ctx: 8 (over z, x), fsdp: 4 (over y, core).
Axes of the slice: x: 2, y: 2, z: 4, core: 2. Of those that a mesh axis runs over, the one named last changes fastest.
Arguments:
- layer_input: bfloat16 [2, 4, 1024, 1024], P(None, 'fsdp', 'ctx'), may hold values from -6 to 6
- segments: int32 [2, 4, 1024], P(None, 'fsdp', 'ctx'), may hold values from 0 to 15, never falling along the last dimension, each value on 1 to 512 neighbouring positions
- cotangent: bfloat16 [2, 4, 1024, 1024], P(None, 'fsdp', 'ctx'), may hold values from -6 to 6
- query_weight: bfloat16 [1024, 1024], P('fsdp'), may hold values from -0.1875 to 0.1875
- key_weight: bfloat16 [1024, 1024], P('fsdp'), may hold values from -0.1875 to 0.1875
- value_weight: bfloat16 [1024, 1024], P('fsdp'), may hold values from -0.1875 to 0.1875
- output_weight: bfloat16 [1024, 1024], P('fsdp'), may hold values from -0.75 to 0.75
- expand_weight: bfloat16 [1024, 4096], P('fsdp'), may hold values from -0.1875 to 0.1875
- contract_weight: bfloat16 [4096, 1024], P('fsdp'), may hold values from -0.09375 to 0.09375
- query_bias: bfloat16 [1024], P('fsdp'), may hold values from -3 to 3
- value_bias: bfloat16 [1024], P('fsdp'), may hold values from -3 to 3
- output_bias: bfloat16 [1024], P('fsdp'), may hold values from -3 to 3
- first_gain: bfloat16 [1024], P('fsdp'), may hold values from 0.099609375 to 1.8984375
- first_shift: bfloat16 [1024], P('fsdp'), may hold values from -3 to 3
- expand_bias: bfloat16 [4096], P('fsdp'), may hold values from -3 to 3
- contract_bias: bfloat16 [1024], P('fsdp'), may hold values from -3 to 3
- second_gain: bfloat16 [1024], P('fsdp'), may hold values from 0.099609375 to 1.8984375
- second_shift: bfloat16 [1024], P('fsdp'), may hold values from -3 to 3
Outputs:
- layer_output: bfloat16 [2, 4, 1024, 1024], P(None, 'fsdp', 'ctx')
- input_grad: float32 [2, 4, 1024, 1024], P(None, 'fsdp', 'ctx')
- query_weight_grad: float32 [1024, 1024], P('fsdp')
- key_weight_grad: float32 [1024, 1024], P('fsdp')
- value_weight_grad: float32 [1024, 1024], P('fsdp')
- output_weight_grad: float32 [1024, 1024], P('fsdp')
- expand_weight_grad: float32 [1024, 4096], P('fsdp')
- contract_weight_grad: float32 [4096, 1024], P('fsdp')
- query_bias_grad: float32 [1024], P('fsdp')
- value_bias_grad: float32 [1024], P('fsdp')
- output_bias_grad: float32 [1024], P('fsdp')
- first_gain_grad: float32 [1024], P('fsdp')
- first_shift_grad: float32 [1024], P('fsdp')
- expand_bias_grad: float32 [4096], P('fsdp')
- contract_bias_grad: float32 [1024], P('fsdp')
- second_gain_grad: float32 [1024], P('fsdp')
- second_shift_grad: float32 [1024], P('fsdp')
Inputs may be any that keep to these rules, and one draw needn't show every extreme that they name: `segments`: in each sequence the ids never fall along the positions; each document holds 1 to 512 positions, and one holds exactly 512.
All inputs are finite; a program needn't handle non-finite values.
Results may differ from a plain program's by a relative error of at most 0.025.
Values may be sent and summed in bfloat16 or wider, within the bound.
A program may use at most 192 MiB of HBM per device.

v0:
```python
import jax
import jax.numpy as jnp
from jax import lax
from jax.sharding import PartitionSpec as P

HEADS = 16
HEAD_DIM = 64


def as_sent(x):
    return jax.tree.map(lambda a: a.astype(jnp.bfloat16) if a.dtype == jnp.float32 else a, x)


def plain_dot(left_side, right_side):
    return jnp.dot(left_side, right_side, preferred_element_type=jnp.float32)


def left_dot(left_side, right_side):
    return lax.dot_general(
        left_side, right_side, (((0,), (0,)), ((), ())), preferred_element_type=jnp.float32
    )


def right_dot(left_side, right_side):
    return lax.dot_general(
        left_side, right_side, (((1,), (1,)), ((), ())), preferred_element_type=jnp.float32
    )


def norm_forward(hidden, gain_row, offset_row):
    centre = hidden - jnp.mean(hidden, axis=-1, keepdims=True)
    inverse = lax.rsqrt(jnp.mean(centre * centre, axis=-1, keepdims=True) + 1e-05)
    normed = centre * inverse
    return (normed * gain_row.astype(jnp.float32) + offset_row.astype(jnp.float32), normed, inverse)


def norm_backward(grad_out, normed, inverse, gain_row):
    scaled = grad_out * gain_row.astype(jnp.float32)
    grad_in = inverse * (
        scaled
        - jnp.mean(scaled, axis=-1, keepdims=True)
        - normed * jnp.mean(scaled * normed, axis=-1, keepdims=True)
    )
    return (grad_in, jnp.sum(grad_out * normed, axis=0), jnp.sum(grad_out, axis=0))


def gather_weights(shards):
    return (
        lax.all_gather(shards[0], "fsdp", axis=0, tiled=True),
        lax.all_gather(shards[1], "fsdp", axis=0, tiled=True),
        lax.all_gather(shards[2], "fsdp", axis=0, tiled=True),
        lax.all_gather(shards[3], "fsdp", axis=0, tiled=True),
        lax.all_gather(shards[4], "fsdp", axis=0, tiled=True),
        lax.all_gather(shards[5], "fsdp", axis=0, tiled=True),
        lax.all_gather(shards[6], "fsdp", axis=0, tiled=True),
        lax.all_gather(shards[7], "fsdp", axis=0, tiled=True),
        lax.all_gather(shards[8], "fsdp", axis=0, tiled=True),
        lax.all_gather(shards[9], "fsdp", axis=0, tiled=True),
        lax.all_gather(shards[10], "fsdp", axis=0, tiled=True),
        lax.all_gather(shards[11], "fsdp", axis=0, tiled=True),
        lax.all_gather(shards[12], "fsdp", axis=0, tiled=True),
        lax.all_gather(shards[13], "fsdp", axis=0, tiled=True),
        lax.all_gather(shards[14], "fsdp", axis=0, tiled=True),
    )


def attend_forward(query_bf, key_bf, value_bf, seg_local):
    row_count = query_bf.shape[0]
    score_scale = HEAD_DIM ** (-0.5)
    query_heads = query_bf.reshape(row_count, HEADS, HEAD_DIM)
    run_max = jnp.full((HEADS, row_count), -1e30, jnp.float32)
    key_rows = lax.all_gather(key_bf, "ctx", axis=0, tiled=True)
    value_rows = lax.all_gather(value_bf, "ctx", axis=0, tiled=True)
    key_seg = lax.all_gather(seg_local, "ctx", axis=0, tiled=True)
    piece_rows = key_rows.shape[0]
    key_heads = key_rows.reshape(piece_rows, HEADS, HEAD_DIM)
    value_heads = value_rows.reshape(piece_rows, HEADS, HEAD_DIM)
    scores = (
        jnp.einsum("rhd,khd->hrk", query_heads, key_heads, preferred_element_type=jnp.float32)
        * score_scale
    )
    same_doc = seg_local[:, None] == key_seg[None, :]
    scores = jnp.where(same_doc[None], scores, -1e30)
    new_max = jnp.maximum(run_max, jnp.max(scores, axis=-1))
    numerators = jnp.exp(scores - new_max[..., None])
    run_sum = jnp.sum(numerators, axis=-1)
    accumulated = jnp.einsum(
        "hrk,khd->hrd",
        numerators.astype(jnp.bfloat16),
        value_heads,
        preferred_element_type=jnp.float32,
    )
    run_max, run_sum, accumulated = (new_max, run_sum, accumulated)
    context = jnp.transpose(accumulated / run_sum[..., None], (1, 0, 2)).reshape(
        row_count, HEADS * HEAD_DIM
    )
    return (context, run_max + jnp.log(run_sum))


def block_grads(
    query_heads, grad_heads, query_seg, log_sum, row_delta, key_heads, value_heads, key_seg
):
    score_scale = HEAD_DIM ** (-0.5)
    scores = (
        jnp.einsum("rhd,khd->hrk", query_heads, key_heads, preferred_element_type=jnp.float32)
        * score_scale
    )
    same_doc = query_seg[:, None] == key_seg[None, :]
    scores = jnp.where(same_doc[None], scores, -1e30)
    probs_full = jnp.exp(scores - log_sum[..., None])
    grad_probs = jnp.einsum(
        "rhd,khd->hrk", grad_heads, value_heads, preferred_element_type=jnp.float32
    )
    grad_scores = (probs_full * (grad_probs - row_delta[..., None])).astype(jnp.bfloat16)
    return (probs_full, grad_scores)


def attend_backward(query_bf, key_bf, value_bf, seg_local, context, log_sum, grad_context):
    row_count = query_bf.shape[0]
    score_scale = HEAD_DIM ** (-0.5)
    key_every, value_every, seg_every = (
        lax.all_gather(key_bf, "ctx", axis=0, tiled=True),
        lax.all_gather(value_bf, "ctx", axis=0, tiled=True),
        lax.all_gather(seg_local, "ctx", axis=0, tiled=True),
    )
    length = key_every.shape[0]
    block_len = min(512, length)
    query_heads = query_bf.reshape(row_count, HEADS, HEAD_DIM)
    grad_heads = grad_context.reshape(row_count, HEADS, HEAD_DIM)
    row_delta = jnp.sum(
        (grad_context.astype(jnp.float32) * context).reshape(row_count, HEADS, HEAD_DIM), axis=-1
    ).T

    def visit_block(grad_query, block_num):
        first_row = block_num * block_len
        key_heads = lax.dynamic_slice_in_dim(key_every, first_row, block_len, 0).reshape(
            block_len, HEADS, HEAD_DIM
        )
        value_heads = lax.dynamic_slice_in_dim(value_every, first_row, block_len, 0).reshape(
            block_len, HEADS, HEAD_DIM
        )
        key_seg = lax.dynamic_slice_in_dim(seg_every, first_row, block_len, 0)
        probs_full, grad_scores = block_grads(
            query_heads, grad_heads, seg_local, log_sum, row_delta, key_heads, value_heads, key_seg
        )
        grad_query = (
            grad_query
            + jnp.einsum("hrk,khd->rhd", grad_scores, key_heads, preferred_element_type=jnp.float32)
            * score_scale
        )
        grad_keys = (
            jnp.einsum("hrk,rhd->khd", grad_scores, query_heads, preferred_element_type=jnp.float32)
            * score_scale
        )
        grad_values = jnp.einsum(
            "hrk,rhd->khd",
            probs_full.astype(jnp.bfloat16),
            grad_heads,
            preferred_element_type=jnp.float32,
        )
        stacked = jnp.stack(
            (
                grad_keys.reshape(block_len, HEADS * HEAD_DIM),
                grad_values.reshape(block_len, HEADS * HEAD_DIM),
            ),
            axis=1,
        )
        return (grad_query, stacked)

    grad_query, pieces = lax.scan(
        visit_block,
        jnp.zeros((row_count, HEADS, HEAD_DIM), jnp.float32),
        jnp.arange(length // block_len),
    )
    key_terms = pieces.reshape(length, 2, HEADS * HEAD_DIM)
    own_rows = lax.psum_scatter(
        key_terms.astype(jnp.bfloat16), "ctx", scatter_dimension=0, tiled=True
    ).astype(jnp.float32)
    grad_keyed = own_rows[:, 0].astype(jnp.bfloat16)
    grad_valued = own_rows[:, 1].astype(jnp.bfloat16)
    grad_queries = grad_query.reshape(row_count, HEADS * HEAD_DIM).astype(jnp.bfloat16)
    return (grad_queries, grad_keyed, grad_valued)


def layer_forward(inputs, seg_local, full_weights):
    (
        query_weight,
        key_weight,
        value_weight,
        output_weight,
        expand_weight,
        contract_weight,
        query_bias,
        value_bias,
        output_bias,
        first_gain,
        first_shift,
        expand_bias,
        contract_bias,
        second_gain,
        second_shift,
    ) = full_weights
    query_bf = (plain_dot(inputs, query_weight) + query_bias.astype(jnp.float32)).astype(
        jnp.bfloat16
    )
    key_bf = plain_dot(inputs, key_weight).astype(jnp.bfloat16)
    value_bf = (plain_dot(inputs, value_weight) + value_bias.astype(jnp.float32)).astype(
        jnp.bfloat16
    )
    context, log_sum = attend_forward(query_bf, key_bf, value_bf, seg_local)
    context_bf = context.astype(jnp.bfloat16)
    first_sum = (
        inputs.astype(jnp.float32)
        + plain_dot(context_bf, output_weight)
        + output_bias.astype(jnp.float32)
    )
    first_out, normed_one, inverse_one = norm_forward(first_sum, first_gain, first_shift)
    first_bf = first_out.astype(jnp.bfloat16)
    hidden = plain_dot(first_bf, expand_weight) + expand_bias.astype(jnp.float32)
    gelled_bf = jax.nn.gelu(hidden, approximate=False).astype(jnp.bfloat16)
    second_sum = (
        first_out + plain_dot(gelled_bf, contract_weight) + contract_bias.astype(jnp.float32)
    )
    result, normed_two, inverse_two = norm_forward(second_sum, second_gain, second_shift)
    kept_state = (
        query_bf,
        key_bf,
        value_bf,
        context,
        log_sum,
        context_bf,
        normed_one,
        inverse_one,
        first_bf,
        hidden,
        gelled_bf,
        normed_two,
        inverse_two,
    )
    return (result.astype(jnp.bfloat16), kept_state)


def layer_backward(inputs, seg_local, grad_out, kept_state, full_weights):
    (
        query_weight,
        key_weight,
        value_weight,
        output_weight,
        expand_weight,
        contract_weight,
        query_bias,
        value_bias,
        output_bias,
        first_gain,
        first_shift,
        expand_bias,
        contract_bias,
        second_gain,
        second_shift,
    ) = full_weights
    (
        query_bf,
        key_bf,
        value_bf,
        context,
        log_sum,
        context_bf,
        normed_one,
        inverse_one,
        first_bf,
        hidden,
        gelled_bf,
        normed_two,
        inverse_two,
    ) = kept_state
    grad_second, second_gain_grad, second_shift_grad = norm_backward(
        grad_out.astype(jnp.float32), normed_two, inverse_two, second_gain
    )
    grad_branch = grad_second.astype(jnp.bfloat16)
    contract_weight_grad = left_dot(gelled_bf, grad_branch)
    contract_bias_grad = jnp.sum(grad_branch.astype(jnp.float32), axis=0)
    grad_gelled = right_dot(grad_branch, contract_weight)
    gelu_pull = jax.vjp(lambda values: jax.nn.gelu(values, approximate=False), hidden)[1]
    grad_hidden = gelu_pull(grad_gelled)[0].astype(jnp.bfloat16)
    expand_weight_grad = left_dot(first_bf, grad_hidden)
    expand_bias_grad = jnp.sum(grad_hidden.astype(jnp.float32), axis=0)
    grad_first = grad_second + right_dot(grad_hidden, expand_weight)
    grad_attn, first_gain_grad, first_shift_grad = norm_backward(
        grad_first, normed_one, inverse_one, first_gain
    )
    grad_attn_low = grad_attn.astype(jnp.bfloat16)
    output_weight_grad = left_dot(context_bf, grad_attn_low)
    output_bias_grad = jnp.sum(grad_attn_low.astype(jnp.float32), axis=0)
    grad_context = right_dot(grad_attn_low, output_weight).astype(jnp.bfloat16)
    grad_queries, grad_keyed, grad_valued = attend_backward(
        query_bf, key_bf, value_bf, seg_local, context, log_sum, grad_context
    )
    query_weight_grad = left_dot(inputs, grad_queries)
    key_weight_grad = left_dot(inputs, grad_keyed)
    value_weight_grad = left_dot(inputs, grad_valued)
    query_bias_grad = jnp.sum(grad_queries.astype(jnp.float32), axis=0)
    value_bias_grad = jnp.sum(grad_valued.astype(jnp.float32), axis=0)
    grad_input = (
        grad_attn
        + right_dot(grad_queries, query_weight)
        + right_dot(grad_keyed, key_weight)
        + right_dot(grad_valued, value_weight)
    )
    grad_terms = (
        query_weight_grad,
        key_weight_grad,
        value_weight_grad,
        output_weight_grad,
        expand_weight_grad,
        contract_weight_grad,
        query_bias_grad,
        value_bias_grad,
        output_bias_grad,
        first_gain_grad,
        first_shift_grad,
        expand_bias_grad,
        contract_bias_grad,
        second_gain_grad,
        second_shift_grad,
    )
    return (grad_input, grad_terms)


def per_device(
    layer_input,
    segments,
    cotangent,
    query_weight,
    key_weight,
    value_weight,
    output_weight,
    expand_weight,
    contract_weight,
    query_bias,
    value_bias,
    output_bias,
    first_gain,
    first_shift,
    expand_bias,
    contract_bias,
    second_gain,
    second_shift,
):
    shards = (
        query_weight,
        key_weight,
        value_weight,
        output_weight,
        expand_weight,
        contract_weight,
        query_bias,
        value_bias,
        output_bias,
        first_gain,
        first_shift,
        expand_bias,
        contract_bias,
        second_gain,
        second_shift,
    )
    micro_count = layer_input.shape[0]
    results = []
    grad_inputs = []
    totals = None
    for micro_step in range(micro_count):
        inputs = layer_input[micro_step, 0]
        seg_local = segments[micro_step, 0].astype(jnp.bfloat16)
        front_weights = gather_weights(shards)
        result, kept_state = layer_forward(inputs, seg_local, front_weights)
        behind = gather_weights(shards)
        grad_input, grad_terms = layer_backward(
            inputs, seg_local, cotangent[micro_step, 0], kept_state, behind
        )
        results.append(result)
        grad_inputs.append(grad_input)
        if totals is None:
            totals = grad_terms
        else:
            totals = tuple(
                (left_side + right_side for left_side, right_side in zip(totals, grad_terms))
            )
    reduced = jax.tree.map(
        lambda part: part.astype(jnp.float32),
        lax.psum_scatter(as_sent(totals), "fsdp", scatter_dimension=0, tiled=True),
    )
    summed = jax.tree.map(lambda part: part.astype(jnp.float32), lax.psum(as_sent(reduced), "ctx"))
    layer_output = jnp.stack(results, axis=0)[:, None]
    input_grad = jnp.stack(grad_inputs, axis=0)[:, None]
    return (
        layer_output,
        input_grad,
        summed[0],
        summed[1],
        summed[2],
        summed[3],
        summed[4],
        summed[5],
        summed[6],
        summed[7],
        summed[8],
        summed[9],
        summed[10],
        summed[11],
        summed[12],
        summed[13],
        summed[14],
    )


def solution(mesh):
    in_specs = (
        P(None, "fsdp", "ctx", None),
        P(None, "fsdp", "ctx"),
        P(None, "fsdp", "ctx", None),
        P("fsdp", None),
        P("fsdp", None),
        P("fsdp", None),
        P("fsdp", None),
        P("fsdp", None),
        P("fsdp", None),
        P("fsdp"),
        P("fsdp"),
        P("fsdp"),
        P("fsdp"),
        P("fsdp"),
        P("fsdp"),
        P("fsdp"),
        P("fsdp"),
        P("fsdp"),
    )
    out_specs = (
        P(None, "fsdp", "ctx", None),
        P(None, "fsdp", "ctx", None),
        P("fsdp", None),
        P("fsdp", None),
        P("fsdp", None),
        P("fsdp", None),
        P("fsdp", None),
        P("fsdp", None),
        P("fsdp"),
        P("fsdp"),
        P("fsdp"),
        P("fsdp"),
        P("fsdp"),
        P("fsdp"),
        P("fsdp"),
        P("fsdp"),
        P("fsdp"),
    )
    return jax.shard_map(
        per_device, mesh=mesh, in_specs=in_specs, out_specs=out_specs, check_vma=False
    )
```

profile of v0, /device:TPU:0, one launch (start us, length us, event | category | flops | bytes accessed | tf_op | source)
XLA Modules:
  0.0 1220.2 jit_solution(14195021096110765214)
XLA Ops:
  10.1 6.0 all-gather.3
  16.1 18.8 %all-gather.27.cloned.1.call-done = bf16[1024,1024]{1,0:T(8,128)(2,1)} async-done(((bf16[256,1024]{1,0:T(8,128)(2,1)}), bf16[1024,1024]{1,0:T(8,128)(2,1)}) %all-gather.27.cloned.1.call-update) | async-done | bytes 2097168 | tf_op jit(solution)/shard_map/all_gather | solution.py:51
  37.8 21.3 %all-gather.23.cloned.1.call-done = bf16[1024,1024]{1,0:T(8,128)(2,1)} async-done(((bf16[256,1024]{1,0:T(8,128)(2,1)}), bf16[1024,1024]{1,0:T(8,128)(2,1)}) %all-gather.23.cloned.1.call-update) | async-done | bytes 2097168 | tf_op jit(solution)/shard_map/all_gather | solution.py:50
  68.2 5.1 all-gather.7
  73.3 5.2 all_gather.55
  78.4 5.1 all-gather.4
  83.5 5.1 all-gather.2
  88.6 5.1 all-gather.6
  93.7 5.1 all-gather.5
  98.8 5.1 all-gather.8
  103.9 20.6 %all-gather = bf16[1,1,1024]{2,1,0:T(2,128)(2,1)S(1)} all-gather(bf16[1,1,128]{2,1,0:T(2,128)(2,1)S(1)} %get-tuple-element.466), channel_id=2, replica_groups=mesh['ctx'=8,'fsdp'=4] {'ctx'}, dimensions={2}, use_global_device_ids=true | all-gather | bytes 2304 | tf_op jit(solution)/shard_map/all_gather | solution.py:74
  124.6 16.3 %all-gather.1 = bf16[1,1,1024]{2,1,0:T(2,128)(2,1)S(1)} all-gather(bf16[1,1,128]{2,1,0:T(2,128)(2,1)S(1)} %get-tuple-element.465), channel_id=3, replica_groups=mesh['ctx'=8,'fsdp'=4] {'ctx'}, dimensions={2}, use_global_device_ids=true | all-gather | bytes 2304 | tf_op jit(solution)/shard_map/all_gather | solution.py:74
  140.9 5.4 all-gather.9
  150.3 4.0 copy.99
  154.3 31.3 %all-gather.25.cloned.1.call-done = bf16[1024,1024]{1,0:T(8,128)(2,1)} async-done(((bf16[128,1024]{1,0:T(8,128)(2,1)}), bf16[1024,1024]{1,0:T(8,128)(2,1)}) %all-gather.25.cloned.1.call-update) | async-done | bytes 2097168 | tf_op jit(solution)/shard_map/all_gather | solution.py:72
  185.6 3.9 copy.98
  199.6 36.4 %all-gather.39.cloned.1.call-done = bf16[1024,1024]{1,0:T(8,128)(2,1)} async-done(((bf16[128,1024]{1,0:T(8,128)(2,1)}), bf16[1024,1024]{1,0:T(8,128)(2,1)}) %all-gather.39.cloned.1.call-update) | async-done | bytes 2097168 | tf_op jit(solution)/shard_map/all_gather | solution.py:73
  236.0 3.9 copy.102
  239.9 46.6 %all-gather.37.cloned.1.call-done = bf16[1024,1024]{1,0:T(8,128)(2,1)} async-done(((bf16[128,1024]{1,0:T(8,128)(2,1)}), bf16[1024,1024]{1,0:T(8,128)(2,1)}) %all-gather.37.cloned.1.call-update) | async-done | bytes 2097168 | tf_op jit(solution)/shard_map/all_gather | solution.py:72
  286.5 3.9 copy.101
  290.4 18.7 %all-gather.31.cloned.1.call-done = bf16[1024,1024]{1,0:T(8,128)(2,1)} async-done(((bf16[256,1024]{1,0:T(8,128)(2,1)}), bf16[1024,1024]{1,0:T(8,128)(2,1)}) %all-gather.31.cloned.1.call-update) | async-done | bytes 2097168 | tf_op jit(solution)/shard_map/all_gather | solution.py:52
  317.0 4.4 fusion.71
  323.0 46.0 %all-gather.33.cloned.1.call-done = bf16[1024,4096]{1,0:T(8,128)(2,1)} async-done(((bf16[256,4096]{1,0:T(8,128)(2,1)}), bf16[1024,4096]{1,0:T(8,128)(2,1)}) %all-gather.33.cloned.1.call-update) | async-done | bytes 8388624 | tf_op jit(solution)/shard_map/all_gather | solution.py:53
  369.1 6.1 convolution_add_fusion.1
  375.2 53.7 %all-gather.35.cloned.1.call-done = bf16[4096,1024]{1,0:T(8,128)(2,1)} async-done(((bf16[1024,1024]{1,0:T(8,128)(2,1)}), bf16[4096,1024]{1,0:T(8,128)(2,1)}) %all-gather.35.cloned.1.call-update) | async-done | bytes 8388624 | tf_op jit(solution)/shard_map/all_gather | solution.py:54
  428.9 9.7 fusion.170
  442.2 5.7 fusion.172
  451.1 8.1 convert_reduce_fusion.1
  462.9 8.1 convert_reduce_fusion
  471.0 4.4 convert_reduce_fusion.7
  479.9 34.4 %while.26 = (s32[]{:T(128)}, f32[128,16,64]{0,2,1:T(8,128)}, bf16[2,512,2,1024]{3,1,0,2:T(8,128)(2,1)}, s32[2]{0:T(128)S(1)}, bf16[1024,1024]{0,1:T(8,128)(2,1)}...) while((s32[]{:T(128)}, f32[128,16,64]{0,2,1:T(8,128)}, ...), condition=%wide.region_18.19_spmd.clone, body=%wide.region_17.18_spmd.clone.sunk | while | flops 684130304 | bytes 77819448 | solution.py:170
  523.5 34.9 %while.27 = (s32[]{:T(128)}, f32[128,16,64]{0,2,1:T(8,128)}, bf16[2,512,2,1024]{3,1,0,2:T(8,128)(2,1)}, s32[2]{0:T(128)S(1)}, bf16[1024,1024]{0,1:T(8,128)(2,1)}...) while((s32[]{:T(128)}, f32[128,16,64]{0,2,1:T(8,128)}, ...), condition=%wide.region_26.27_spmd.clone, body=%wide.region_25.26_spmd.clone.sunk | while | flops 684130304 | bytes 77819448 | solution.py:170
  566.6 35.8 %reduce-scatter.9.cloned.1.call-done = bf16[128,2,1024]{2,0,1:T(8,128)(2,1)} async-done(((bf16[1024,2,1024]{2,0,1:T(8,128)(2,1)}), bf16[128,2,1024]{2,0,1:T(8,128)(2,1)}) %reduce-scatter.9.cloned.1.call-update) | async-done | bytes 524304 | tf_op jit(solution)/shard_map/reduce_scatter | solution.py:176
  602.4 3.7 fusion.111
  606.1 88.5 %reduce-scatter.11.cloned.1.call-done = bf16[128,2,1024]{2,0,1:T(8,128)(2,1)} async-done(((bf16[1024,2,1024]{2,0,1:T(8,128)(2,1)}), bf16[128,2,1024]{2,0,1:T(8,128)(2,1)}) %reduce-scatter.11.cloned.1.call-update) | async-done | bytes 524304 | tf_op jit(solution)/shard_map/reduce_scatter | solution.py:176
  694.7 4.3 fusion.53
  704.2 8.2 fusion.164
  712.5 11.8 add_convert_fusion.1
  725.9 10.9 fusion.148
  736.8 12.7 %add_convert_fusion = bf16[4096,1024]{1,0:T(8,128)(2,1)} fusion(f32[4096,1024]{1,0:T(8,128)} %fusion.148, f32[128,1024]{1,0:T(8,128)S(1)} %copy-done.51, f32[128,4096]{1,0:T(8,128)S(1)} %copy-done.46), kind=kOutput, calls=%fused_computation.44 | convolution fusion | flops 1116340224 | bytes 27787264 | tf_op jit(solution)/shard_map/dot_general | solution.py:19
  749.9 12.6 %reduce-scatter.19.cloned.1.call-done = bf16[256,1024]{1,0:T(8,128)(2,1)} async-done(((bf16[1024,1024]{1,0:T(8,128)(2,1)}), bf16[256,1024]{1,0:T(8,128)(2,1)}) %reduce-scatter.19.cloned.1.call-update) | async-done | bytes 524304 | tf_op jit(solution)/shard_map/reduce_scatter | solution.py:389
  762.4 34.4 %reduce-scatter.15.cloned.1.call-done = bf16[256,1024]{0,1:T(8,128)(2,1)} async-done(((bf16[1024,1024]{0,1:T(8,128)(2,1)}), bf16[256,1024]{0,1:T(8,128)(2,1)}) %reduce-scatter.15.cloned.1.call-update) | async-done | bytes 524304 | tf_op jit(solution)/shard_map/reduce_scatter | solution.py:389
  796.8 34.6 %reduce-scatter.17.cloned.1.call-done = bf16[256,1024]{0,1:T(8,128)(2,1)} async-done(((bf16[1024,1024]{0,1:T(8,128)(2,1)}), bf16[256,1024]{0,1:T(8,128)(2,1)}) %reduce-scatter.17.cloned.1.call-update) | async-done | bytes 524304 | tf_op jit(solution)/shard_map/reduce_scatter | solution.py:389
  831.4 74.2 %reduce-scatter.21.cloned.1.call-done = bf16[256,4096]{1,0:T(8,128)(2,1)} async-done(((bf16[1024,4096]{1,0:T(8,128)(2,1)}), bf16[256,4096]{1,0:T(8,128)(2,1)}) %reduce-scatter.21.cloned.1.call-update) | async-done | bytes 2097168 | tf_op jit(solution)/shard_map/reduce_scatter | solution.py:389
  905.6 74.4 %reduce-scatter.23.cloned.1.call-done = bf16[1024,1024]{1,0:T(8,128)(2,1)} async-done(((bf16[4096,1024]{1,0:T(8,128)(2,1)}), bf16[1024,1024]{1,0:T(8,128)(2,1)}) %reduce-scatter.23.cloned.1.call-update) | async-done | bytes 2097168 | tf_op jit(solution)/shard_map/reduce_scatter | solution.py:389
  990.1 11.3 all-reduce.11
  1002.0 23.1 %all-reduce.9 = (bf16[256]{0:T(256)(128)(2,1)S(1)}, bf16[256]{0:T(256)(128)(2,1)S(1)}, bf16[256]{0:T(256)(128)(2,1)S(1)}, bf16[256]{0:T(256)(128)(2,1)S(1)}, bf1...) all-reduce(bf16[256]{0:T(256)(128)(2,1)S(1)} %dynamic-slice.1, ...), channel_id=1, replica_groups=mesh['ctx'=8,'fsdp'=4] {'ctx'}, use_global_device_ids=true, to_apply=%region_43.44 | all-reduce | flops 3072 | bytes 12288 | tf_op jit(solution)/shard_map/psum | solution.py:391
  1037.3 164.2 %all-reduce.14.cloned.1.call-done = (bf16[256,1024]{0,1:T(8,128)(2,1)}, bf16[256,1024]{0,1:T(8,128)(2,1)}, bf16[256,1024]{0,1:T(8,128)(2,1)}, bf16[256,1024]{1,0...) async-done(((bf16[256,1024]{0,1:T(8,128)(2,1)}, bf16[256,1024]{0,1:T(8,128)(2,1)}, bf16[256,1024]{0,1:T(8,128)(2,1)}, bf16[256,1024]{1,0:T(8,128)(2,1)}, ...) | async-done | bytes 6291472 | tf_op jit(solution)/shard_map/psum | solution.py:391
  (440 shorter events, 176.4 us)
Async XLA Ops:
  7.2 27.7 %all-gather.27.cloned.1.call-start = ((), (), s32[]{:S(2)}) async-start(), calls=%async_computation.11 | async-start | bytes 2621440 | tf_op jit(solution)/shard_map/all_gather | solution.py:51
  7.9 51.2 %copy-start.13 = (bf16[2,1,128,1024]{3,2,1,0:T(8,128)(2,1)S(1)}, bf16[2,1,128,1024]{3,2,1,0:T(8,128)(2,1)}, u32[]{:S(2)}) copy-start(bf16[2,1,128,1024]{3,2,1,0:T(8,128)(2,1)} %param.22) | copy-start | bytes 1572868
  7.9 51.2 %all-gather.23.cloned.1.call-start = ((), (), s32[]{:S(2)}) async-start(), calls=%async_computation.9 | async-start | bytes 2621440 | tf_op jit(solution)/shard_map/all_gather | solution.py:50
  8.7 138.5 %all-gather.21.cloned.1.call-start = ((), (), s32[]{:S(2)}) async-start(), calls=%async_computation.8 | async-start | bytes 2621440 | tf_op jit(solution)/shard_map/all_gather | solution.py:49
  9.4 140.9 %all-gather.29.cloned.1.call-start = ((), (), s32[]{:S(2)}) async-start(), calls=%async_computation.12 | async-start | bytes 2359296 | tf_op jit(solution)/shard_map/all_gather | solution.py:73
  37.7 24.2 %copy-start.6 = (bf16[1024,1024]{1,0:T(8,128)(2,1)S(1)}, bf16[1024,1024]{1,0:T(8,128)(2,1)}, u32[]{:S(2)}) copy-start(bf16[1024,1024]{1,0:T(8,128)(2,1)} %all-gather.27.cloned.1.call-done) | copy-start | bytes 6291460
  37.8 147.9 %all-gather.25.cloned.1.call-start = ((), (), s32[]{:S(2)}) async-start(), calls=%async_computation.10 | async-start | bytes 2359296 | tf_op jit(solution)/shard_map/all_gather | solution.py:72
  61.9 174.1 %all-gather.39.cloned.1.call-start = ((), (), s32[]{:S(2)}) async-start(), calls=%async_computation.17 | async-start | bytes 2359296 | tf_op jit(solution)/shard_map/all_gather | solution.py:73
  63.1 223.4 %all-gather.37.cloned.1.call-start = ((), (), s32[]{:S(2)}) async-start(), calls=%async_computation.16 | async-start | bytes 2359296 | tf_op jit(solution)/shard_map/all_gather | solution.py:72
  65.9 243.3 %all-gather.31.cloned.1.call-start = ((), (), s32[]{:S(2)}) async-start(), calls=%async_computation.13 | async-start | bytes 2621440 | tf_op jit(solution)/shard_map/all_gather | solution.py:52
  66.7 11.7 copy-start.93
  66.7 16.8 %copy-start.90 = (s32[2,1,128]{2,1,0:T(1,128)S(1)}, s32[2,1,128]{2,1,0:T(1,128)}, u32[]{:S(2)}) copy-start(s32[2,1,128]{2,1,0:T(1,128)} %param.23) | copy-start | bytes 3076
  66.7 16.8 %copy-start.94 = (bf16[256]{0:T(256)(128)(2,1)S(1)}, bf16[256]{0:T(256)(128)(2,1)}, u32[]{:S(2)}) copy-start(bf16[256]{0:T(256)(128)(2,1)} %param.31) | copy-start | bytes 1540
  66.7 21.9 %copy-start.95 = (bf16[256]{0:T(256)(128)(2,1)S(1)}, bf16[256]{0:T(256)(128)(2,1)}, u32[]{:S(2)}) copy-start(bf16[256]{0:T(256)(128)(2,1)} %param.35) | copy-start | bytes 1540
  66.7 27.0 %copy-start.96 = (bf16[256]{0:T(256)(128)(2,1)S(1)}, bf16[256]{0:T(256)(128)(2,1)}, u32[]{:S(2)}) copy-start(bf16[256]{0:T(256)(128)(2,1)} %param.34) | copy-start | bytes 1540
  66.8 32.1 %copy-start.97 = (bf16[256]{0:T(256)(128)(2,1)S(1)}, bf16[256]{0:T(256)(128)(2,1)}, u32[]{:S(2)}) copy-start(bf16[256]{0:T(256)(128)(2,1)} %param.38) | copy-start | bytes 1540
  66.8 74.1 %copy-start.98 = (bf16[256]{0:T(256)(128)(2,1)S(1)}, bf16[256]{0:T(256)(128)(2,1)}, u32[]{:S(2)}) copy-start(bf16[256]{0:T(256)(128)(2,1)} %param.39) | copy-start | bytes 1540
  66.8 302.3 %all-gather.33.cloned.1.call-start = ((), (), s32[]{:S(2)}) async-start(), calls=%async_computation.14 | async-start | bytes 10485760 | tf_op jit(solution)/shard_map/all_gather | solution.py:53
  67.5 361.4 %all-gather.35.cloned.1.call-start = ((), (), s32[]{:S(2)}) async-start(), calls=%async_computation.15 | async-start | bytes 10485760 | tf_op jit(solution)/shard_map/all_gather | solution.py:54
  68.1 534.3 %reduce-scatter.9.cloned.1.call-start = ((), (), s32[]{:S(2)}) async-start(), calls=%async_computation.18 | async-start | bytes 4718592 | tf_op jit(solution)/shard_map/reduce_scatter | solution.py:176
  93.7 346.5 %copy-start.56 = (f32[4,1,256]{2,1,0:T(1,128)}, f32[4,1,256]{2,1,0:T(1,128)S(1)}, u32[]{:S(2)}) copy-start(f32[4,1,256]{2,1,0:T(1,128)S(1)} %convert_element_type.499) | copy-start | bytes 12292
  103.9 46.1 %copy-start.70 = (bf16[128]{0:T(256)(128)(2,1)}, bf16[128]{0:T(256)(128)(2,1)S(1)}, u32[]{:S(2)}) copy-start(bf16[128]{0:T(256)(128)(2,1)S(1)} %get-tuple-element.654) | copy-start | bytes 772
  103.9 46.1 %copy-start.72 = (bf16[128]{0:T(256)(128)(2,1)}, bf16[128]{0:T(256)(128)(2,1)S(1)}, u32[]{:S(2)}) copy-start(bf16[128]{0:T(256)(128)(2,1)S(1)} %get-tuple-element.702) | copy-start | bytes 772
  124.6 25.5 %copy-start.66 = (bf16[1024]{0:T(1024)(128)(2,1)}, bf16[1024]{0:T(1024)(128)(2,1)S(1)}, u32[]{:S(2)}) copy-start(bf16[1024]{0:T(1024)(128)(2,1)S(1)} %reduce.4) | copy-start | bytes 6148
  150.2 161.3 %copy-start.4 = (bf16[128,1024]{0,1:T(8,128)(2,1)}, bf16[128,1024]{0,1:T(8,128)(2,1)S(1)}, u32[]{:S(2)}) copy-start(bf16[128,1024]{0,1:T(8,128)(2,1)S(1)} %copy.100) | copy-start | bytes 786436
  198.6 110.6 %copy-start.31 = (f32[128,16,64]{0,2,1:T(8,128)}, f32[128,16,64]{0,2,1:T(8,128)S(1)}, u32[]{:S(2)}) copy-start(f32[128,16,64]{0,2,1:T(8,128)S(1)} %fusion.74) | copy-start | bytes 1572868
  290.4 21.1 %copy-start.54 = (pred[128,1024]{1,0:T(8,128)(4,1)S(1)}, pred[128,1024]{1,0:T(8,128)(4,1)}, u32[]{:S(2)}) copy-start(pred[128,1024]{1,0:T(8,128)(4,1)} %broadcast_compare_fusion.2) | copy-start | bytes 393220
  311.3 159.6 %copy-start.15 = (f32[128,1024]{1,0:T(8,128)}, f32[128,1024]{1,0:T(8,128)S(1)}, u32[]{:S(2)}) copy-start(f32[128,1024]{1,0:T(8,128)S(1)} %get-tuple-element.470) | copy-start | bytes 1572868
  311.3 159.6 %copy-start.74 = (f32[128]{0:T(128)}, f32[128]{0:T(128)S(1)}, u32[]{:S(2)}) copy-start(f32[128]{0:T(128)S(1)} %broadcast_multiply_fusion.11) | copy-start | bytes 1540
  323.0 148.0 %copy-start.76 = (f32[128]{0:T(128)}, f32[128]{0:T(128)S(1)}, u32[]{:S(2)}) copy-start(f32[128]{0:T(128)S(1)} %add_rsqrt_fusion.3) | copy-start | bytes 1540
  428.9 9.9 slice-start
  428.9 9.9 slice-start.1
  428.9 9.9 copy-start.18
  442.2 20.6 %copy-start.45 = (f32[128,4096]{1,0:T(8,128)}, f32[128,4096]{1,0:T(8,128)S(1)}, u32[]{:S(2)}) copy-start(f32[128,4096]{1,0:T(8,128)S(1)} %convolution_add_fusion) | copy-start | bytes 6291460
  451.1 19.9 %copy-start.50 = (f32[128,1024]{1,0:T(8,128)}, f32[128,1024]{1,0:T(8,128)S(1)}, u32[]{:S(2)}) copy-start(f32[128,1024]{1,0:T(8,128)S(1)} %get-tuple-element.439) | copy-start | bytes 1572868
  514.4 180.3 %reduce-scatter.11.cloned.1.call-start = ((), (), s32[]{:S(2)}) async-start(), calls=%async_computation.19 | async-start | bytes 4718592 | tf_op jit(solution)/shard_map/reduce_scatter | solution.py:176
  558.4 191.5 %reduce-scatter.13.cloned.1.call-start = ((), (), s32[]{:S(2)}) async-start(), calls=%async_computation.20 | async-start | bytes 2621440 | tf_op jit(solution)/shard_map/reduce_scatter | solution.py:389
  562.7 199.7 %reduce-scatter.19.cloned.1.call-start = ((), (), s32[]{:S(2)}) async-start(), calls=%async_computation.23 | async-start | bytes 2621440 | tf_op jit(solution)/shard_map/reduce_scatter | solution.py:389
  566.6 230.2 %reduce-scatter.15.cloned.1.call-start = ((), (), s32[]{:S(2)}) async-start(), calls=%async_computation.21 | async-start | bytes 2621440 | tf_op jit(solution)/shard_map/reduce_scatter | solution.py:389
  699.0 132.4 %reduce-scatter.17.cloned.1.call-start = ((), (), s32[]{:S(2)}) async-start(), calls=%async_computation.22 | async-start | bytes 2621440 | tf_op jit(solution)/shard_map/reduce_scatter | solution.py:389
  702.9 9.6 copy-start.20
  702.9 202.7 %reduce-scatter.21.cloned.1.call-start = ((), (), s32[]{:S(2)}) async-start(), calls=%async_computation.24 | async-start | bytes 10485760 | tf_op jit(solution)/shard_map/reduce_scatter | solution.py:389
  724.3 255.6 %reduce-scatter.23.cloned.1.call-start = ((), (), s32[]{:S(2)}) async-start(), calls=%async_computation.25 | async-start | bytes 10485760 | tf_op jit(solution)/shard_map/reduce_scatter | solution.py:389
  725.9 10.9 copy-start.46
  725.9 10.9 copy-start.51
  749.6 451.9 %all-reduce.14.cloned.1.call-start = ((), (), s32[]{:S(2)}) async-start(), calls=%async_computation.26 | async-start | bytes 12582912 | tf_op jit(solution)/shard_map/psum | solution.py:391
  990.0 42.9 %copy-start.7 = (bf16[1024,1024]{1,0:T(8,128)(2,1)S(1)}, bf16[1024,1024]{1,0:T(8,128)(2,1)}, u32[]{:S(2)}) copy-start(bf16[1024,1024]{1,0:T(8,128)(2,1)} %all-gather.27.cloned.1.call-done) | copy-start | bytes 6291460
  990.0 42.9 %copy-start.41 = (bf16[128,2,1024]{2,0,1:T(8,128)(2,1)S(1)}, bf16[128,2,1024]{2,0,1:T(8,128)(2,1)}, u32[]{:S(2)}) copy-start(bf16[128,2,1024]{2,0,1:T(8,128)(2,1)} %reduce-scatter.11.cloned.1.call-done) | copy-start | bytes 1572868
  (79 other events, 239.4 us)
Sparse Core Ops, SparseCore 0:
  9.6 25.2 all-gather.26
  36.5 22.5 all-gather.22
  60.7 22.6 all-gather.20
  85.9 49.3 all-gather.28
  137.8 47.7 all-gather.24
  188.2 47.7 all-gather.38
  238.7 47.7 all-gather.36
  288.1 21.0 all-gather.30
  310.8 58.2 all-gather.32
  370.5 58.3 all-gather.34
  514.5 87.8 reduce-scatter.8
  606.9 87.6 reduce-scatter.10
  697.2 31.1 reduce-scatter.12
  730.9 31.4 reduce-scatter.18
  765.4 31.4 reduce-scatter.14
  799.9 31.3 reduce-scatter.16
  833.8 71.7 reduce-scatter.20
  908.2 71.6 reduce-scatter.22
  984.9 216.5 all-reduce.13
where the time goes:
time: 1230 us; the launch traced here: 1220 us
  waiting for transfers between devices  796 us (65%)
  matrix products  178 us (14%)
  blocking collectives  118 us (10%)
  local copies, waits for them, and re-layouts  74.1 us (6%)
  other arithmetic  32.8 us (3%)
  between operations  16.8 us (1%)
    reduce_scatter x6, waiting for transfers between devices, per_device(): lax.psum_scatter(as_sent(totals), 'fsdp', scatter_dimension=0, tiled=True)  230 us
    psum x1, waiting for transfers between devices, per_device(): lax.psum(as_sent(reduced), 'ctx')  164 us
    reduce_scatter x2, waiting for transfers between devices, attend_backward(): lax.psum_scatter(key_terms.astype(jnp.bfloat16), 'ctx', scatter_dimension...  124 us
    all_gather x2, waiting for transfers between devices, attend_forward(): key_rows = lax.all_gather(key_bf, 'ctx', axis=0, tiled=True)  77.9 us
    dot_general x12, matrix products, left_dot(): lax.dot_general(left_side, right_side, (((0,), (0,)), ((), ())), preferre...  60 us
    all_gather x1, waiting for transfers between devices, gather_weights(): lax.all_gather(shards[5], 'fsdp', axis=0, tiled=True)  53.7 us
    all_gather x1, waiting for transfers between devices, gather_weights(): lax.all_gather(shards[4], 'fsdp', axis=0, tiled=True)  46 us
    dot_general x12, matrix products, plain_dot(): return jnp.dot(left_side, right_side, preferred_element_type=jnp.float32)  37.6 us
  transfers between devices with their start and end apart: 19, of which 16 were waited for; matrix products, arithmetic and copies ran while one was open for 15% of the time, Pallas kernels for 0%

commit v1 on v0

--- a/solution.py
+++ b/solution.py
@@ -71,7 +71,12 @@
     run_max = jnp.full((HEADS, row_count), -1e30, jnp.float32)
     key_rows = lax.all_gather(key_bf, "ctx", axis=0, tiled=True)
     value_rows = lax.all_gather(value_bf, "ctx", axis=0, tiled=True)
-    key_seg = lax.all_gather(seg_local, "ctx", axis=0, tiled=True)
+    ring = [seg_local]
+    for hop in range(7):
+        ring.append(lax.ppermute(ring[-1], "ctx", [(dev, (dev + 1) % 8) for dev in range(8)]))
+    key_seg = jnp.roll(
+        jnp.concatenate(ring[::-1], axis=0), (lax.axis_index("ctx") + 1) * ring[0].shape[0], axis=0
+    )
     piece_rows = key_rows.shape[0]
     key_heads = key_rows.reshape(piece_rows, HEADS, HEAD_DIM)
     value_heads = value_rows.reshape(piece_rows, HEADS, HEAD_DIM)

time: 1230 us -> 1230 us (level)
    ppermute x0 -> x14, waiting for transfers between devices: none -> 36.6 us  [attend_forward(): lax.ppermute(ring[-1], 'ctx', [(dev, (dev + 1) % 8) for dev in range(8)])]
    all_gather x2, waiting for transfers between devices: 77.9 us -> 51 us  [attend_forward(): key_rows = lax.all_gather(key_bf, 'ctx', axis=0, tiled=True)]
    reduce_scatter x2, waiting for transfers between devices: 124 us -> 104 us  [attend_backward(): lax.psum_scatter(key_terms.astype(jnp.bfloat16), 'ctx', scatter_dimension...]
  transfers between devices with their start and end apart: 19 -> 33, of which waited for: 16 -> 27; matrix products, arithmetic and copies ran while one was open for 15% -> 15% of each run, Pallas kernels for 0% -> 0%
where the time goes in v1:
time: 1230 us; the launch traced here: 1220 us
  waiting for transfers between devices  786 us (64%)
  matrix products  178 us (14%)
  blocking collectives  121 us (10%)
  local copies, waits for them, and re-layouts  77.1 us (6%)
  other arithmetic  33 us (3%)
  between operations  16.9 us (1%)
    reduce_scatter x6, waiting for transfers between devices, per_device(): lax.psum_scatter(as_sent(totals), 'fsdp', scatter_dimension=0, tiled=True)  230 us
    psum x1, waiting for transfers between devices, per_device(): lax.psum(as_sent(reduced), 'ctx')  164 us
    reduce_scatter x2, waiting for transfers between devices, attend_backward(): lax.psum_scatter(key_terms.astype(jnp.bfloat16), 'ctx', scatter_dimension...  104 us
    dot_general x12, matrix products, left_dot(): lax.dot_general(left_side, right_side, (((0,), (0,)), ((), ())), preferre...  60.1 us
    all_gather x1, waiting for transfers between devices, gather_weights(): lax.all_gather(shards[5], 'fsdp', axis=0, tiled=True)  53.8 us
    all_gather x2, waiting for transfers between devices, attend_forward(): key_rows = lax.all_gather(key_bf, 'ctx', axis=0, tiled=True)  51 us
    all_gather x1, waiting for transfers between devices, gather_weights(): lax.all_gather(shards[4], 'fsdp', axis=0, tiled=True)  46.6 us
    all_gather x2, blocking collectives, attend_backward(): lax.all_gather(seg_local, 'ctx', axis=0, tiled=True)  40.3 us
  transfers between devices with their start and end apart: 33, of which 27 were waited for; matrix products, arithmetic and copies ran while one was open for 15% of the time, Pallas kernels for 0%

profile of v1, /device:TPU:0, one launch (start us, length us, event | category | flops | bytes accessed | tf_op | source)
XLA Modules:
  0.0 1220.7 jit_solution(4448056189988579757)
XLA Ops:
  10.1 6.0 all-gather.3
  16.1 18.8 %all-gather.27.cloned.1.call-done = bf16[1024,1024]{1,0:T(8,128)(2,1)} async-done(((bf16[256,1024]{1,0:T(8,128)(2,1)}), bf16[1024,1024]{1,0:T(8,128)(2,1)}) %all-gather.27.cloned.1.call-update) | async-done | bytes 2097168 | tf_op jit(solution)/shard_map/all_gather | solution.py:51
  37.8 21.3 %all-gather.23.cloned.1.call-done = bf16[1024,1024]{1,0:T(8,128)(2,1)} async-done(((bf16[256,1024]{1,0:T(8,128)(2,1)}), bf16[1024,1024]{1,0:T(8,128)(2,1)}) %all-gather.23.cloned.1.call-update) | async-done | bytes 2097168 | tf_op jit(solution)/shard_map/all_gather | solution.py:50
  71.8 5.1 all-gather.7
  76.8 5.1 all-gather.4
  81.9 5.1 all-gather.2
  87.0 5.1 all-gather.6
  92.0 5.1 all-gather.5
  97.1 5.1 all-gather.8
  102.1 5.1 all-gather.9
  107.2 19.5 %all-gather = bf16[1,1,1024]{2,1,0:T(2,128)(2,1)S(1)} all-gather(bf16[1,1,128]{2,1,0:T(2,128)(2,1)S(1)} %get-tuple-element.464), channel_id=2, replica_groups=mesh['ctx'=8,'fsdp'=4] {'ctx'}, dimensions={2}, use_global_device_ids=true | all-gather | bytes 2304 | tf_op jit(solution)/shard_map/all_gather | solution.py:129
  126.7 5.1 all_gather.54
  132.1 6.0 collective-permute-done.1
  138.2 6.1 collective-permute-done.2
  144.5 6.1 collective-permute-done.3
  150.7 6.1 collective-permute-done.4
  156.9 6.1 collective-permute-done.5
  163.7 5.6 collective-permute-done.6
  180.6 4.5 all-gather.25.cloned.1.call-done
  199.0 37.0 %all-gather.39.cloned.1.call-done = bf16[1024,1024]{1,0:T(8,128)(2,1)} async-done(((bf16[128,1024]{1,0:T(8,128)(2,1)}), bf16[1024,1024]{1,0:T(8,128)(2,1)}) %all-gather.39.cloned.1.call-update) | async-done | bytes 2097168 | tf_op jit(solution)/shard_map/all_gather | solution.py:73
  239.9 46.6 %all-gather.37.cloned.1.call-done = bf16[1024,1024]{1,0:T(8,128)(2,1)} async-done(((bf16[128,1024]{1,0:T(8,128)(2,1)}), bf16[1024,1024]{1,0:T(8,128)(2,1)}) %all-gather.37.cloned.1.call-update) | async-done | bytes 2097168 | tf_op jit(solution)/shard_map/all_gather | solution.py:72
  290.6 18.6 %all-gather.31.cloned.1.call-done = bf16[1024,1024]{1,0:T(8,128)(2,1)} async-done(((bf16[256,1024]{1,0:T(8,128)(2,1)}), bf16[1024,1024]{1,0:T(8,128)(2,1)}) %all-gather.31.cloned.1.call-update) | async-done | bytes 2097168 | tf_op jit(solution)/shard_map/all_gather | solution.py:52
  322.5 46.6 %all-gather.33.cloned.1.call-done = bf16[1024,4096]{1,0:T(8,128)(2,1)} async-done(((bf16[256,4096]{1,0:T(8,128)(2,1)}), bf16[1024,4096]{1,0:T(8,128)(2,1)}) %all-gather.33.cloned.1.call-update) | async-done | bytes 8388624 | tf_op jit(solution)/shard_map/all_gather | solution.py:53
  369.1 6.1 convolution_add_fusion.1
  375.1 53.8 %all-gather.35.cloned.1.call-done = bf16[4096,1024]{1,0:T(8,128)(2,1)} async-done(((bf16[1024,1024]{1,0:T(8,128)(2,1)}), bf16[4096,1024]{1,0:T(8,128)(2,1)}) %all-gather.35.cloned.1.call-update) | async-done | bytes 8388624 | tf_op jit(solution)/shard_map/all_gather | solution.py:54
  428.9 9.7 fusion.173
  442.2 5.9 fusion.175
  451.3 8.1 convert_reduce_fusion.1
  463.1 8.1 convert_reduce_fusion
  471.2 4.4 convert_reduce_fusion.7
  480.1 34.4 %while.26 = (s32[]{:T(128)}, f32[128,16,64]{0,2,1:T(8,128)}, bf16[2,512,2,1024]{3,1,0,2:T(8,128)(2,1)}, s32[2]{0:T(128)S(1)}, bf16[1024,1024]{0,1:T(8,128)(2,1)}...) while((s32[]{:T(128)}, f32[128,16,64]{0,2,1:T(8,128)}, ...), condition=%wide.region_18.20_spmd.clone, body=%wide.region_17.19_spmd.clone.sunk | while | flops 684130304 | bytes 77819448 | solution.py:175
  515.2 20.8 %all-gather.1 = bf16[1,1,1024]{2,1,0:T(2,128)(2,1)S(1)} all-gather(bf16[1,1,128]{2,1,0:T(2,128)(2,1)S(1)} %copy-done.86), channel_id=3, replica_groups=mesh['ctx'=8,'fsdp'=4] {'ctx'}, dimensions={2}, use_global_device_ids=true | all-gather | bytes 2304 | tf_op jit(solution)/shard_map/all_gather | solution.py:129
  544.1 34.6 %while.27 = (s32[]{:T(128)}, f32[128,16,64]{0,2,1:T(8,128)}, bf16[2,512,2,1024]{3,1,0,2:T(8,128)(2,1)}, s32[2]{0:T(128)S(1)}, bf16[1024,1024]{0,1:T(8,128)(2,1)}...) while((s32[]{:T(128)}, f32[128,16,64]{0,2,1:T(8,128)}, ...), condition=%wide.region_26.28_spmd.clone, body=%wide.region_25.27_spmd.clone.sunk | while | flops 684130304 | bytes 77819448 | solution.py:175
  587.1 15.8 %reduce-scatter.9.cloned.1.call-done = bf16[128,2,1024]{2,0,1:T(8,128)(2,1)} async-done(((bf16[1024,2,1024]{2,0,1:T(8,128)(2,1)}), bf16[128,2,1024]{2,0,1:T(8,128)(2,1)}) %reduce-scatter.9.cloned.1.call-update) | async-done | bytes 524304 | tf_op jit(solution)/shard_map/reduce_scatter | solution.py:181
  606.5 88.7 %reduce-scatter.11.cloned.1.call-done = bf16[128,2,1024]{2,0,1:T(8,128)(2,1)} async-done(((bf16[1024,2,1024]{2,0,1:T(8,128)(2,1)}), bf16[128,2,1024]{2,0,1:T(8,128)(2,1)}) %reduce-scatter.11.cloned.1.call-update) | async-done | bytes 524304 | tf_op jit(solution)/shard_map/reduce_scatter | solution.py:181
  695.2 4.3 fusion.53
  704.9 8.2 fusion.166
  713.1 11.9 add_convert_fusion.1
  726.5 10.9 fusion.150
  737.5 12.7 %add_convert_fusion = bf16[4096,1024]{1,0:T(8,128)(2,1)} fusion(f32[4096,1024]{1,0:T(8,128)} %fusion.150, f32[128,1024]{1,0:T(8,128)S(1)} %copy-done.51, f32[128,4096]{1,0:T(8,128)S(1)} %copy-done.46), kind=kOutput, calls=%fused_computation.44 | convolution fusion | flops 1116340224 | bytes 27787264 | tf_op jit(solution)/shard_map/dot_general | solution.py:19
  750.5 12.5 %reduce-scatter.19.cloned.1.call-done = bf16[256,1024]{1,0:T(8,128)(2,1)} async-done(((bf16[1024,1024]{1,0:T(8,128)(2,1)}), bf16[256,1024]{1,0:T(8,128)(2,1)}) %reduce-scatter.19.cloned.1.call-update) | async-done | bytes 524304 | tf_op jit(solution)/shard_map/reduce_scatter | solution.py:394
  763.0 34.4 %reduce-scatter.15.cloned.1.call-done = bf16[256,1024]{0,1:T(8,128)(2,1)} async-done(((bf16[1024,1024]{0,1:T(8,128)(2,1)}), bf16[256,1024]{0,1:T(8,128)(2,1)}) %reduce-scatter.15.cloned.1.call-update) | async-done | bytes 524304 | tf_op jit(solution)/shard_map/reduce_scatter | solution.py:394
  797.4 34.6 %reduce-scatter.17.cloned.1.call-done = bf16[256,1024]{0,1:T(8,128)(2,1)} async-done(((bf16[1024,1024]{0,1:T(8,128)(2,1)}), bf16[256,1024]{0,1:T(8,128)(2,1)}) %reduce-scatter.17.cloned.1.call-update) | async-done | bytes 524304 | tf_op jit(solution)/shard_map/reduce_scatter | solution.py:394
  831.9 74.2 %reduce-scatter.21.cloned.1.call-done = bf16[256,4096]{1,0:T(8,128)(2,1)} async-done(((bf16[1024,4096]{1,0:T(8,128)(2,1)}), bf16[256,4096]{1,0:T(8,128)(2,1)}) %reduce-scatter.21.cloned.1.call-update) | async-done | bytes 2097168 | tf_op jit(solution)/shard_map/reduce_scatter | solution.py:394
  906.2 74.4 %reduce-scatter.23.cloned.1.call-done = bf16[1024,1024]{1,0:T(8,128)(2,1)} async-done(((bf16[4096,1024]{1,0:T(8,128)(2,1)}), bf16[1024,1024]{1,0:T(8,128)(2,1)}) %reduce-scatter.23.cloned.1.call-update) | async-done | bytes 2097168 | tf_op jit(solution)/shard_map/reduce_scatter | solution.py:394
  990.7 11.3 all-reduce.11
  1002.6 23.1 %all-reduce.9 = (bf16[256]{0:T(256)(128)(2,1)S(1)}, bf16[256]{0:T(256)(128)(2,1)S(1)}, bf16[256]{0:T(256)(128)(2,1)S(1)}, bf16[256]{0:T(256)(128)(2,1)S(1)}, bf1...) all-reduce(bf16[256]{0:T(256)(128)(2,1)S(1)} %dynamic-slice.1, ...), channel_id=1, replica_groups=mesh['ctx'=8,'fsdp'=4] {'ctx'}, use_global_device_ids=true, to_apply=%region_43.45 | all-reduce | flops 3072 | bytes 12288 | tf_op jit(solution)/shard_map/psum | solution.py:396
  1037.9 164.1 %all-reduce.14.cloned.1.call-done = (bf16[256,1024]{0,1:T(8,128)(2,1)}, bf16[256,1024]{0,1:T(8,128)(2,1)}, bf16[256,1024]{0,1:T(8,128)(2,1)}, bf16[256,1024]{1,0...) async-done(((bf16[256,1024]{0,1:T(8,128)(2,1)}, bf16[256,1024]{0,1:T(8,128)(2,1)}, bf16[256,1024]{0,1:T(8,128)(2,1)}, bf16[256,1024]{1,0:T(8,128)(2,1)}, ...) | async-done | bytes 6291472 | tf_op jit(solution)/shard_map/psum | solution.py:396
  (482 shorter events, 207.4 us)
Async XLA Ops:
  7.2 27.7 %all-gather.27.cloned.1.call-start = ((), (), s32[]{:S(2)}) async-start(), calls=%async_computation.11 | async-start | bytes 2621440 | tf_op jit(solution)/shard_map/all_gather | solution.py:51
  7.9 51.2 %copy-start.13 = (bf16[2,1,128,1024]{3,2,1,0:T(8,128)(2,1)S(1)}, bf16[2,1,128,1024]{3,2,1,0:T(8,128)(2,1)}, u32[]{:S(2)}) copy-start(bf16[2,1,128,1024]{3,2,1,0:T(8,128)(2,1)} %param.24) | copy-start | bytes 1572868
  7.9 51.2 %all-gather.23.cloned.1.call-start = ((), (), s32[]{:S(2)}) async-start(), calls=%async_computation.9 | async-start | bytes 2621440 | tf_op jit(solution)/shard_map/all_gather | solution.py:50
  8.7 164.8 %all-gather.21.cloned.1.call-start = ((), (), s32[]{:S(2)}) async-start(), calls=%async_computation.8 | async-start | bytes 2621440 | tf_op jit(solution)/shard_map/all_gather | solution.py:49
  9.4 167.1 %all-gather.29.cloned.1.call-start = ((), (), s32[]{:S(2)}) async-start(), calls=%async_computation.12 | async-start | bytes 2359296 | tf_op jit(solution)/shard_map/all_gather | solution.py:73
  37.7 24.2 %copy-start.6 = (bf16[1024,1024]{1,0:T(8,128)(2,1)S(1)}, bf16[1024,1024]{1,0:T(8,128)(2,1)}, u32[]{:S(2)}) copy-start(bf16[1024,1024]{1,0:T(8,128)(2,1)} %all-gather.27.cloned.1.call-done) | copy-start | bytes 6291460
  37.8 147.3 %all-gather.25.cloned.1.call-start = ((), (), s32[]{:S(2)}) async-start(), calls=%async_computation.10 | async-start | bytes 2359296 | tf_op jit(solution)/shard_map/all_gather | solution.py:72
  61.9 174.1 %all-gather.39.cloned.1.call-start = ((), (), s32[]{:S(2)}) async-start(), calls=%async_computation.17 | async-start | bytes 2359296 | tf_op jit(solution)/shard_map/all_gather | solution.py:73
  63.1 223.4 %all-gather.37.cloned.1.call-start = ((), (), s32[]{:S(2)}) async-start(), calls=%async_computation.16 | async-start | bytes 2359296 | tf_op jit(solution)/shard_map/all_gather | solution.py:72
  65.9 243.3 %all-gather.31.cloned.1.call-start = ((), (), s32[]{:S(2)}) async-start(), calls=%async_computation.13 | async-start | bytes 2621440 | tf_op jit(solution)/shard_map/all_gather | solution.py:52
  66.8 59.9 %copy-start.85 = (bf16[1024]{0:T(1024)(128)(2,1)S(1)}, bf16[1024]{0:T(1024)(128)(2,1)}, u32[]{:S(2)}) copy-start(bf16[1024]{0:T(1024)(128)(2,1)} %param.38) | copy-start | bytes 6148
  66.8 302.3 %all-gather.33.cloned.1.call-start = ((), (), s32[]{:S(2)}) async-start(), calls=%async_computation.14 | async-start | bytes 10485760 | tf_op jit(solution)/shard_map/all_gather | solution.py:53
  67.5 361.4 %all-gather.35.cloned.1.call-start = ((), (), s32[]{:S(2)}) async-start(), calls=%async_computation.15 | async-start | bytes 10485760 | tf_op jit(solution)/shard_map/all_gather | solution.py:54
  68.1 534.8 %reduce-scatter.9.cloned.1.call-start = ((), (), s32[]{:S(2)}) async-start(), calls=%async_computation.18 | async-start | bytes 4718592 | tf_op jit(solution)/shard_map/reduce_scatter | solution.py:181
  68.7 107.6 %copy-start.64 = (bf16[128]{0:T(256)(128)(2,1)}, bf16[128]{0:T(256)(128)(2,1)S(1)}, u32[]{:S(2)}) copy-start(bf16[128]{0:T(256)(128)(2,1)S(1)} %get-tuple-element.655) | copy-start | bytes 772
  68.7 107.6 %copy-start.66 = (bf16[128]{0:T(256)(128)(2,1)}, bf16[128]{0:T(256)(128)(2,1)S(1)}, u32[]{:S(2)}) copy-start(bf16[128]{0:T(256)(128)(2,1)S(1)} %get-tuple-element.703) | copy-start | bytes 772
  68.7 63.2 %collective-permute-start = (bf16[128]{0:T(256)(128)(2,1)S(1)}, bf16[128]{0:T(256)(128)(2,1)S(1)}, u32[]{:S(2)}, u32[]{:S(2)}) collective-permute-start(bf16[128]{0:T(256)(128)(2,1)S(1)} %get-tuple-element.703), channel_id=1, source_target_pairs={{0,4},{4,8},{8,12},{12,16},{16,20},{20,24},{24,28},{28,0},{1,5},{5... | collective-permute-start | bytes 776 | tf_op jit(solution)/shard_map/ppermute | solution.py:76
  70.2 61.7 %collective-permute-start.7 = (bf16[128]{0:T(256)(128)(2,1)S(1)}, bf16[128]{0:T(256)(128)(2,1)S(1)}, u32[]{:S(2)}, u32[]{:S(2)}) collective-permute-start(bf16[128]{0:T(256)(128)(2,1)S(1)} %get-tuple-element.655), channel_id=1, source_target_pairs={{0,4},{4,8},{8,12},{12,16},{16,20},{20,24},{24,28},{28,0},{1,5},{5... | collective-permute-start | bytes 776 | tf_op jit(solution)/shard_map/ppermute | solution.py:76
  131.9 6.2 collective-permute-start.1
  131.9 6.3 collective-permute-start.8
  138.1 6.2 collective-permute-start.2
  138.2 6.2 collective-permute-start.9
  144.3 6.2 collective-permute-start.3
  144.4 6.2 collective-permute-start.10
  150.6 6.2 collective-permute-start.4
  150.6 289.6 %copy-start.56 = (f32[4,1,256]{2,1,0:T(1,128)}, f32[4,1,256]{2,1,0:T(1,128)S(1)}, u32[]{:S(2)}) copy-start(f32[4,1,256]{2,1,0:T(1,128)S(1)} %convert_element_type.499) | copy-start | bytes 12292
  150.7 6.2 collective-permute-start.11
  156.8 6.2 collective-permute-start.5
  156.9 6.2 collective-permute-start.12
  163.0 6.3 collective-permute-start.6
  163.2 7.6 collective-permute-start.13
  176.5 135.1 %copy-start.4 = (bf16[128,1024]{0,1:T(8,128)(2,1)}, bf16[128,1024]{0,1:T(8,128)(2,1)S(1)}, u32[]{:S(2)}) copy-start(bf16[128,1024]{0,1:T(8,128)(2,1)S(1)} %copy.100) | copy-start | bytes 786436
  198.0 111.2 %copy-start.31 = (f32[128,16,64]{0,2,1:T(8,128)}, f32[128,16,64]{0,2,1:T(8,128)S(1)}, u32[]{:S(2)}) copy-start(f32[128,16,64]{0,2,1:T(8,128)S(1)} %fusion.74) | copy-start | bytes 1572868
  311.3 159.9 %copy-start.15 = (f32[128,1024]{1,0:T(8,128)}, f32[128,1024]{1,0:T(8,128)S(1)}, u32[]{:S(2)}) copy-start(f32[128,1024]{1,0:T(8,128)S(1)} %get-tuple-element.471) | copy-start | bytes 1572868
  311.3 159.8 %copy-start.70 = (f32[128]{0:T(128)}, f32[128]{0:T(128)S(1)}, u32[]{:S(2)}) copy-start(f32[128]{0:T(128)S(1)} %broadcast_multiply_fusion.11) | copy-start | bytes 1540
  322.4 148.7 %copy-start.72 = (f32[128]{0:T(128)}, f32[128]{0:T(128)S(1)}, u32[]{:S(2)}) copy-start(f32[128]{0:T(128)S(1)} %add_rsqrt_fusion.3) | copy-start | bytes 1540
  514.5 22.5 %copy-start.19 = (f32[128,1024]{1,0:T(8,128)S(1)}, f32[128,1024]{1,0:T(8,128)}, u32[]{:S(2)}) copy-start(f32[128,1024]{1,0:T(8,128)} %copy-done.17) | copy-start | bytes 1572868
  514.6 23.8 %copy-start.12 = (bf16[1024,1024]{1,0:T(8,128)(2,1)S(1)}, bf16[1024,1024]{1,0:T(8,128)(2,1)}, u32[]{:S(2)}) copy-start(bf16[1024,1024]{1,0:T(8,128)(2,1)} %all-gather.31.cloned.1.call-done) | copy-start | bytes 6291460
  514.6 180.7 %reduce-scatter.11.cloned.1.call-start = ((), (), s32[]{:S(2)}) async-start(), calls=%async_computation.19 | async-start | bytes 4718592 | tf_op jit(solution)/shard_map/reduce_scatter | solution.py:181
  578.8 171.7 %reduce-scatter.13.cloned.1.call-start = ((), (), s32[]{:S(2)}) async-start(), calls=%async_computation.20 | async-start | bytes 2621440 | tf_op jit(solution)/shard_map/reduce_scatter | solution.py:394
  583.1 179.9 %reduce-scatter.19.cloned.1.call-start = ((), (), s32[]{:S(2)}) async-start(), calls=%async_computation.23 | async-start | bytes 2621440 | tf_op jit(solution)/shard_map/reduce_scatter | solution.py:394
  587.0 210.4 %reduce-scatter.15.cloned.1.call-start = ((), (), s32[]{:S(2)}) async-start(), calls=%async_computation.21 | async-start | bytes 2621440 | tf_op jit(solution)/shard_map/reduce_scatter | solution.py:394
  699.6 132.3 %reduce-scatter.17.cloned.1.call-start = ((), (), s32[]{:S(2)}) async-start(), calls=%async_computation.22 | async-start | bytes 2621440 | tf_op jit(solution)/shard_map/reduce_scatter | solution.py:394
  703.5 202.7 %reduce-scatter.21.cloned.1.call-start = ((), (), s32[]{:S(2)}) async-start(), calls=%async_computation.24 | async-start | bytes 10485760 | tf_op jit(solution)/shard_map/reduce_scatter | solution.py:394
  725.0 255.6 %reduce-scatter.23.cloned.1.call-start = ((), (), s32[]{:S(2)}) async-start(), calls=%async_computation.25 | async-start | bytes 10485760 | tf_op jit(solution)/shard_map/reduce_scatter | solution.py:394
  750.2 451.9 %all-reduce.14.cloned.1.call-start = ((), (), s32[]{:S(2)}) async-start(), calls=%async_computation.26 | async-start | bytes 12582912 | tf_op jit(solution)/shard_map/psum | solution.py:396
  990.5 42.9 %copy-start.7 = (bf16[1024,1024]{1,0:T(8,128)(2,1)S(1)}, bf16[1024,1024]{1,0:T(8,128)(2,1)}, u32[]{:S(2)}) copy-start(bf16[1024,1024]{1,0:T(8,128)(2,1)} %all-gather.27.cloned.1.call-done) | copy-start | bytes 6291460
  990.5 42.9 %copy-start.41 = (bf16[128,2,1024]{2,0,1:T(8,128)(2,1)S(1)}, bf16[128,2,1024]{2,0,1:T(8,128)(2,1)}, u32[]{:S(2)}) copy-start(bf16[128,2,1024]{2,0,1:T(8,128)(2,1)} %reduce-scatter.11.cloned.1.call-done) | copy-start | bytes 1572868
  (90 other events, 432.1 us)
Sparse Core Ops, SparseCore 0:
  9.6 25.2 all-gather.26
  36.5 22.5 all-gather.22
  60.7 22.6 all-gather.20
  85.9 49.3 all-gather.28
  137.8 47.2 all-gather.24
  187.6 48.3 all-gather.38
  238.7 47.7 all-gather.36
  288.0 21.0 all-gather.30
  310.7 58.2 all-gather.32
  370.5 58.3 all-gather.34
  514.7 88.1 reduce-scatter.8
  607.4 87.8 reduce-scatter.10
  697.8 31.1 reduce-scatter.12
  731.5 31.3 reduce-scatter.18
  765.9 31.4 reduce-scatter.14
  800.5 31.3 reduce-scatter.16
  834.4 71.7 reduce-scatter.20
  908.8 71.7 reduce-scatter.22
  985.5 216.4 all-reduce.13
